TPU v7x, 512 devices: a whole 4x8x8 slice. The times are simulated.
512 devices in a mesh: dp: 32 (over x, z), tp: 16 (over y, core).
Axes of the slice: x: 4, y: 8, z: 8, core: 2. Of those that a mesh axis runs over, the one named last changes fastest.
Arguments:
- queries: bfloat16 [1024, 128, 576], P(('dp', 'tp')), may hold values from -40 to 40
- latent_cache: bfloat16 [1024, 256, 576], P(('dp', 'tp')), may hold values from -5 to 5
- lengths: int32 [1024], P(('dp', 'tp')), may hold values from 1 to 256, 65536 in all
- value_weight: bfloat16 [128, 512, 128], P('tp'), may hold values from -0.25 to 0.25
- output_weight: bfloat16 [16384, 7168], P('tp', 'dp'), may hold values from -0.046875 to 0.046875
Outputs:
- attended: bfloat16 [1024, 7168], P(('dp', 'tp'))
All inputs are finite; a program needn't handle non-finite values. No bound on the sum of `lengths` on one device may be relied on, other than what follows from the above.
Results may differ from a plain program's by a relative error of at most 0.0065.
Values may be sent and summed in bfloat16 or wider, within the bound.
No kernel may reach another device: no remote copies, remote signals or barrier semaphores. Data moves between devices by JAX's collectives and lax.ppermute only.
A program may use at most 64 MiB of HBM per device.

v0:
```python
import jax
import jax.numpy as jnp
from jax import lax
from jax.sharding import PartitionSpec as P

score_scale = 192.0 ** (-0.5)


def local(queries, latent_cache, lengths, value_weight, output_weight):
    requests = queries.shape[0]
    groups = lax.axis_size("tp")
    columns = lax.axis_size("dp")
    latent_width = value_weight.shape[1]
    scores = (
        jnp.einsum("rhe,rje->rhj", queries, latent_cache, preferred_element_type=jnp.float32)
        * score_scale
    )
    alive_mask = lax.broadcasted_iota(jnp.int32, scores.shape, 2) < lengths[:, None, None]
    scores = jnp.where(alive_mask, scores, -1e30)
    row_max = jnp.max(scores, axis=2, keepdims=True)
    powers = jnp.exp(scores - row_max)
    weights = (powers / jnp.sum(powers, axis=2, keepdims=True)).astype(jnp.bfloat16)
    mixture = jnp.einsum("rhj,rje->rhe", weights, latent_cache, preferred_element_type=jnp.float32)
    latent = mixture[:, :, :latent_width].astype(jnp.bfloat16)
    swapped = lax.all_to_all(latent, "tp", split_axis=1, concat_axis=0, tiled=True)
    local_heads = swapped.shape[1]
    stacked = swapped.reshape(groups, requests, local_heads, latent_width)
    everyone = lax.all_gather(stacked, "dp", axis=1, tiled=True)
    values = jnp.einsum(
        "gqhd,hde->gqhe", everyone, value_weight, preferred_element_type=jnp.float32
    )
    values = values.astype(jnp.bfloat16)
    all_values = values.reshape(groups * columns * requests, -1)
    summed = lax.psum_scatter(
        jnp.dot(all_values, output_weight, preferred_element_type=jnp.float32),
        "tp",
        scatter_dimension=0,
        tiled=True,
    )
    rounded = summed.astype(jnp.bfloat16)
    return lax.all_to_all(rounded, "dp", split_axis=0, concat_axis=1, tiled=True)


def solution(mesh):
    return jax.shard_map(
        local,
        mesh=mesh,
        in_specs=(
            P(("dp", "tp"), None, None),
            P(("dp", "tp"), None, None),
            P(("dp", "tp")),
            P("tp", None, None),
            P("tp", "dp"),
        ),
        out_specs=P(("dp", "tp"), None),
        check_vma=False,
    )
```

profile of v0, /device:TPU:2, one launch (start us, length us, event | category | flops | bytes accessed | tf_op | source)
XLA Modules:
  0.0 230.4 jit_solution(6659828259434857418)
XLA Ops:
  6.5 0.0 copy-start
  6.5 0.0 all-gather.2.cloned.1.call-start
  6.5 1.5 fusion.10
  8.1 0.2 fusion.15
  8.3 1.6 fusion.12
  9.9 0.3 copy.11
  10.2 18.2 %all_to_all.34 = bf16[2,128,512]{2,0,1:T(2,128)(2,1)S(1)} all-to-all(bf16[2,128,512]{2,0,1:T(2,128)(2,1)S(1)} %copy.11), channel_id=1, replica_groups=mesh['dp'=32,'tp'=16] {'tp'}, dimensions={1} | all-to-all | bytes 524288 | tf_op jit(solution)/shard_map/all_to_all | solution.py:25
  28.4 0.7 copy.27
  29.1 0.0 all-gather.2.cloned.1.call-update
  29.1 0.0 reduce-scatter.2.cloned.1.call-start
  29.2 104.3 %all-gather.2.cloned.1.call-done = bf16[16,64,8,512]{3,2,0,1:T(8,128)(2,1)} async-done(((bf16[16,2,8,512]{3,2,0,1:T(8,128)(2,1)}), bf16[16,64,8,512]{3,2,0,1:T(8,128)(2,1)}) %all-gather.2.cloned.1.call-update) | async-done | bytes 8388624 | tf_op jit(solution)/shard_map/all_gather | solution.py:28
  133.4 0.0 copy-done
  133.5 8.2 %convert_bitcast_fusion = bf16[16,64,8,128]{3,1,0,2:T(8,128)(2,1)S(1)} fusion(bf16[16,64,8,512]{3,2,0,1:T(8,128)(2,1)} %all-gather.2.cloned.1.call-done, bf16[8,512,128]{2,1,0:T(8,128)(2,1)S(1)} %copy-done), kind=kOutput, calls=%fused_computation.6 | convolution fusion | flops 1074790400 | bytes 11534336 | tf_op jit(solution)/shard_map/gqhd,hde->gqhe/dot_general | solution.py:29
  141.7 0.0 copy-start.1
  141.7 1.8 copy.14
  143.5 0.0 copy-done.1
  143.5 1.7 fusion.3
  145.2 0.0 reduce-scatter.2.cloned.1.call-update
  145.2 57.7 %reduce-scatter.2.cloned.1.call-done = f32[64,224]{1,0:T(8,128)} async-done(((f32[1024,224]{1,0:T(8,128)}), f32[64,224]{1,0:T(8,128)}) %reduce-scatter.2.cloned.1.call-update) | async-done | bytes 57360 | tf_op jit(solution)/shard_map/reduce_scatter | solution.py:34
  202.9 0.8 convert_element_type.16
  203.8 19.0 %all_to_all.35 = bf16[32,2,224]{2,1,0:T(2,128)(2,1)S(1)} all-to-all(bf16[32,2,224]{2,1,0:T(2,128)(2,1)S(1)} %all_to_all.28), channel_id=1, replica_groups=mesh['dp'=32,'tp'=16] {'dp'}, dimensions={0} | all-to-all | bytes 57344 | tf_op jit(solution)/shard_map/all_to_all | solution.py:41
  222.8 0.7 all_to_all.31
  (3 shorter events, 0.1 us)
Async XLA Ops:
  6.5 126.9 %copy-start = (bf16[8,512,128]{2,1,0:T(8,128)(2,1)S(1)}, bf16[8,512,128]{2,1,0:T(8,128)(2,1)}, u32[]{:S(2)}) copy-start(bf16[8,512,128]{2,1,0:T(8,128)(2,1)} %param.8) | copy-start | bytes 3145732
  6.5 126.9 %all-gather.2.cloned.1.call-start = ((), (), s32[]{:S(2)}) async-start(), calls=%async_computation.3 | async-start | bytes 8650752 | tf_op jit(solution)/shard_map/all_gather | solution.py:28
  29.1 173.8 %reduce-scatter.2.cloned.1.call-start = ((), (), s32[]{:S(2)}) async-start(), calls=%async_computation.4 | async-start | bytes 1114112 | tf_op jit(solution)/shard_map/reduce_scatter | solution.py:34
  141.7 1.8 copy-start.1
Sparse Core Ops, SparseCore 0:
  29.3 104.1 all-gather.1
  145.3 57.5 reduce-scatter.1
where the time goes:
time: 231 us; the launch traced here: 230 us
  waiting for transfers between devices  162 us (70%)
  blocking collectives  37.2 us (16%)
  between operations  13.5 us (6%)
  matrix products  13.1 us (6%)
  local copies, waits for them, and re-layouts  3.58 us (2%)
    all_gather x1, waiting for transfers between devices, local(): everyone = lax.all_gather(stacked, 'dp', axis=1, tiled=True)  104 us
    reduce_scatter x1, waiting for transfers between devices, local(): lax.psum_scatter(jnp.dot(all_values, output_weight, preferred_element_typ...  57.7 us
    all_to_all x1, blocking collectives, local(): lax.all_to_all(rounded, 'dp', split_axis=0, concat_axis=1, tiled=True)  19 us
    all_to_all x1, blocking collectives, local(): lax.all_to_all(latent, 'tp', split_axis=1, concat_axis=0, tiled=True)  18.2 us
    dot_general x1, matrix products, local(): jnp.einsum('gqhd,hde->gqhe', everyone, value_weight, preferred_element_ty...  8.21 us
  transfers between devices with their start and end apart: 2, of which 2 were waited for; matrix products, arithmetic and copies ran while one was open for 0% of the time, Pallas kernels for 0%

commit v1 on v0

--- a/solution.py
+++ b/solution.py
@@ -1,9 +1,20 @@
+import functools
 import jax
 import jax.numpy as jnp
 from jax import lax
 from jax.sharding import PartitionSpec as P
 
 score_scale = 192.0 ** (-0.5)
+
+
+def answer_the_roots(field, axis_no):
+    part_now = lax.all_to_all(
+        jnp.stack([field for _ in range(lax.axis_size("dp"))], axis=0), "dp", 0, 0
+    )
+    return jnp.concatenate(part_now, axis=axis_no)
+
+
+pass_spots = functools.partial(answer_the_roots, axis_no=1)
 
 
 def local(queries, latent_cache, lengths, value_weight, output_weight):
@@ -25,7 +36,7 @@
     swapped = lax.all_to_all(latent, "tp", split_axis=1, concat_axis=0, tiled=True)
     local_heads = swapped.shape[1]
     stacked = swapped.reshape(groups, requests, local_heads, latent_width)
-    everyone = lax.all_gather(stacked, "dp", axis=1, tiled=True)
+    everyone = pass_spots(stacked)
     values = jnp.einsum(
         "gqhd,hde->gqhe", everyone, value_weight, preferred_element_type=jnp.float32
     )

time: 231 us -> 345 us (1.49)
  blocking collectives: 37.2 us -> 234 us
  waiting for transfers between devices: 162 us -> 54.4 us
  local copies, waits for them, and re-layouts: 3.58 us -> 30.9 us
    all_to_all x0 -> x1, blocking collectives: none -> 198 us  [answer_the_roots(): lax.all_to_all(jnp.stack([field for _ in range(lax.axis_size('dp'))], axi...]
    all_gather x1 -> x0, waiting for transfers between devices: 104 us -> none  [local(): everyone = lax.all_gather(stacked, 'dp', axis=1, tiled=True)]
    reshape x0 -> x2, local copies, waits for them, and re-layouts: none -> 20 us  [answer_the_roots(): return jnp.concatenate(part_now, axis=axis_no)]
    another operation x0 -> x1, local copies, waits for them, and re-layouts: none -> 7.81 us  [answer_the_roots(): jnp.stack([field for _ in range(lax.axis_size('dp'))], axis=0)]
  transfers between devices with their start and end apart: 2 -> 1, of which waited for: 2 -> 1; matrix products, arithmetic and copies ran while one was open for 0% -> 0% of each run, Pallas kernels for 0% -> 0%
where the time goes in v1:
time: 345 us
  blocking collectives  234 us (68%)
  waiting for transfers between devices  54.4 us (16%)
  local copies, waits for them, and re-layouts  30.9 us (9%)
  between operations  13.5 us (4%)
  matrix products  10.6 us (3%)
    all_to_all x1, blocking collectives, answer_the_roots(): lax.all_to_all(jnp.stack([field for _ in range(lax.axis_size('dp'))], axi...  198 us
    reduce_scatter x1, waiting for transfers between devices, local(): lax.psum_scatter(jnp.dot(all_values, output_weight, preferred_element_typ...  54.4 us
    reshape x2, local copies, waits for them, and re-layouts, answer_the_roots(): return jnp.concatenate(part_now, axis=axis_no)  20 us
    all_to_all x1, blocking collectives, local(): lax.all_to_all(rounded, 'dp', split_axis=0, concat_axis=1, tiled=True)  18.8 us
    all_to_all x1, blocking collectives, local(): lax.all_to_all(latent, 'tp', split_axis=1, concat_axis=0, tiled=True)  18.2 us
    another operation x1, local copies, waits for them, and re-layouts, answer_the_roots(): jnp.stack([field for _ in range(lax.axis_size('dp'))], axis=0)  7.81 us
  transfers between devices with their start and end apart: 1, of which 1 were waited for; matrix products, arithmetic and copies ran while one was open for 0% of the time, Pallas kernels for 0%

profile of v1, /device:TPU:2, one launch (start us, length us, event | category | flops | bytes accessed | tf_op | source)
XLA Modules:
  0.0 344.8 jit_solution(10724854811973056072)
XLA Ops:
  6.5 0.0 copy-start
  6.5 0.0 reduce-scatter.2.cloned.1.call-start
  6.5 1.5 fusion.6
  8.1 0.2 fusion.11
  8.3 1.6 fusion.8
  9.9 0.3 copy.11
  10.2 18.2 %all_to_all.39 = bf16[2,128,512]{2,0,1:T(2,128)(2,1)S(1)} all-to-all(bf16[2,128,512]{2,0,1:T(2,128)(2,1)S(1)} %copy.11), channel_id=1, replica_groups=mesh['dp'=32,'tp'=16] {'tp'}, dimensions={1} | all-to-all | bytes 524288 | tf_op jit(solution)/shard_map/all_to_all | solution.py:36
  28.4 0.2 copy.12
  28.6 7.8 %stack.3 = bf16[32,16,2,8,512]{4,2,1,3,0:T(2,128)(2,1)S(1)} broadcast(bf16[16,2,8,512]{3,1,0,2:T(2,128)(2,1)S(1)} %copy.12), dimensions={1,2,3,4} | broadcast | bytes 8650752 | tf_op jit(solution)/shard_map/stack | solution.py:12
  36.4 197.5 %all_to_all.40 = bf16[32,16,2,8,512]{4,2,1,3,0:T(2,128)(2,1)S(1)} all-to-all(bf16[32,16,2,8,512]{4,2,1,3,0:T(2,128)(2,1)S(1)} %stack.3), channel_id=1, replica_groups=mesh['dp'=32,'tp'=16] {'dp'}, dimensions={0} | all-to-all | bytes 16777216 | tf_op jit(solution)/shard_map/all_to_all | solution.py:11
  233.9 7.0 %copy.13 = bf16[16,32,2,8,512]{4,2,1,0,3:T(2,128)(2,1)} copy(bf16[16,32,2,8,512]{4,2,0,3,1:T(2,128)(2,1)S(1)} %bitcast.26) | data formatting | bytes 16777216 | tf_op jit(solution)/shard_map/reshape | solution.py:14
  240.9 13.1 %reshape.19 = bf16[16,64,8,512]{3,1,0,2:T(8,128)(2,1)} reshape(bf16[16,32,2,8,512]{4,2,1,0,3:T(2,128)(2,1)} %copy.13) | data formatting | bytes 16777216 | tf_op jit(solution)/shard_map/reshape | solution.py:14
  254.0 0.0 copy-done
  254.0 5.7 %convert_bitcast_fusion = bf16[16,64,8,128]{3,1,0,2:T(8,128)(2,1)S(1)} fusion(bf16[16,64,8,512]{3,1,0,2:T(8,128)(2,1)} %reshape.19, bf16[8,512,128]{2,1,0:T(8,128)(2,1)S(1)} %copy-done), kind=kOutput, calls=%fused_computation.4 | convolution fusion | flops 1074790400 | bytes 11534336 | tf_op jit(solution)/shard_map/gqhd,hde->gqhe/dot_general | solution.py:40
  259.7 0.0 copy-start.1
  259.7 1.8 copy.14
  261.5 0.0 copy-done.1
  261.5 1.7 fusion.1
  263.2 0.0 reduce-scatter.2.cloned.1.call-update
  263.2 54.4 %reduce-scatter.2.cloned.1.call-done = f32[64,224]{1,0:T(8,128)} async-done(((f32[1024,224]{1,0:T(8,128)}), f32[64,224]{1,0:T(8,128)}) %reduce-scatter.2.cloned.1.call-update) | async-done | bytes 57360 | tf_op jit(solution)/shard_map/reduce_scatter | solution.py:45
  317.6 0.8 convert_element_type.16
  318.5 18.8 %all_to_all.41 = bf16[32,2,224]{2,1,0:T(2,128)(2,1)S(1)} all-to-all(bf16[32,2,224]{2,1,0:T(2,128)(2,1)S(1)} %all_to_all.32), channel_id=1, replica_groups=mesh['dp'=32,'tp'=16] {'dp'}, dimensions={0} | all-to-all | bytes 57344 | tf_op jit(solution)/shard_map/all_to_all | solution.py:52
  337.3 0.7 all_to_all.35
  (3 shorter events, 0.1 us)
Async XLA Ops:
  6.5 247.4 %copy-start = (bf16[8,512,128]{2,1,0:T(8,128)(2,1)S(1)}, bf16[8,512,128]{2,1,0:T(8,128)(2,1)}, u32[]{:S(2)}) copy-start(bf16[8,512,128]{2,1,0:T(8,128)(2,1)} %param.8) | copy-start | bytes 3145732
  6.5 311.1 %reduce-scatter.2.cloned.1.call-start = ((), (), s32[]{:S(2)}) async-start(), calls=%async_computation.4 | async-start | bytes 1114112 | tf_op jit(solution)/shard_map/reduce_scatter | solution.py:45
  259.7 1.8 copy-start.1
Sparse Core Ops, SparseCore 0:
  263.4 54.1 reduce-scatter.1
